TPU v7x, 32 devices: a whole 2x2x4 slice. The times are simulated.
32 devices in a mesh: group: 4 (over x, core), replica: 8 (over z, y).
Axes of the slice: x: 2, y: 2, z: 4, core: 2. Of those that a mesh axis runs over, the one named last changes fastest.
Arguments:
- activations: float32 [16, 1024, 768], P('replica', 'group'), may hold values from -6 to 6
- out_grad: float32 [16, 1024, 768], P('replica', 'group'), may hold values from -6 to 6
- picture_ids: int32 [16, 1024], P('replica'), may hold values from -1 to 9, as said below
- ln1_gain: float32 [768], P('group'), may hold values from 0.5 to 1.5
- ln1_bias: float32 [768], P('group'), may hold values from -3 to 3
- w_query: float32 [768, 768], P(None, 'group'), may hold values from -0.3125 to 0.3125
- q_bias: float32 [768], P('group'), may hold values from -3 to 3
- w_key: float32 [768, 768], P(None, 'group'), may hold values from -0.3125 to 0.3125
- w_value: float32 [768, 768], P(None, 'group'), may hold values from -0.21875 to 0.21875
- v_bias: float32 [768], P('group'), may hold values from -3 to 3
- w_out: float32 [768, 768], P('group'), may hold values from -1.75 to 1.75
- out_bias: float32 [768], P('group'), may hold values from -3 to 3
- ln2_gain: float32 [768], P('group'), may hold values from 0.5 to 1.5
- ln2_bias: float32 [768], P('group'), may hold values from -3 to 3
- w_fc1: float32 [768, 3072], P(None, 'group'), may hold values from -0.21875 to 0.21875
- fc1_bias: float32 [3072], P('group'), may hold values from -3 to 3
- w_fc2: float32 [3072, 768], P('group'), may hold values from -0.109375 to 0.109375
- fc2_bias: float32 [768], P('group'), may hold values from -3 to 3
Outputs:
- output: float32 [16, 1024, 768], P('replica', 'group')
- grad_input: float32 [16, 1024, 768], P('replica', 'group')
- grad_ln1_gain: float32 [768], P('group')
- grad_ln1_bias: float32 [768], P('group')
- grad_w_query: float32 [768, 768], P(None, 'group')
- grad_q_bias: float32 [768], P('group')
- grad_w_key: float32 [768, 768], P(None, 'group')
- grad_w_value: float32 [768, 768], P(None, 'group')
- grad_v_bias: float32 [768], P('group')
- grad_w_out: float32 [768, 768], P('group')
- grad_out_bias: float32 [768], P('group')
- grad_ln2_gain: float32 [768], P('group')
- grad_ln2_bias: float32 [768], P('group')
- grad_w_fc1: float32 [768, 3072], P(None, 'group')
- grad_fc1_bias: float32 [3072], P('group')
- grad_w_fc2: float32 [3072, 768], P('group')
- grad_fc2_bias: float32 [768], P('group')
Inputs may be any that keep to these rules, and one draw needn't show every extreme that they name: `picture_ids`: each row holds whole pictures numbered 0, 1, 2 and so on from its start, each of 100 to 1024 patches, followed by padding marked -1.
All inputs are finite; a program needn't handle non-finite values.
Results may differ from a plain program's by a relative error of at most 0.04.
Values may be sent and summed in bfloat16 or wider, within the bound.
No kernel may reach another device: no remote copies, remote signals or barrier semaphores. Data moves between devices by JAX's collectives and lax.ppermute only.
A program may use at most 256 MiB of HBM per device.

v0:
```python
import jax
import jax.numpy as jnp
from jax import lax
from jax.sharding import PartitionSpec as P

HEADS = 12
HEAD_DIM = 64


EPS = 1e-06
MASKED = -1e30


def to_float(values):
    return values.astype(jnp.float32)


def normalize(values):
    centred = values - jnp.mean(values, axis=-1, keepdims=True)
    inverse = lax.rsqrt(jnp.mean(centred * centred, axis=-1, keepdims=True) + EPS)
    return (centred * inverse, inverse)


def norm_back(grad_hat, normed_hat, inverse):
    return inverse * (
        grad_hat
        - jnp.mean(grad_hat, axis=-1, keepdims=True)
        - normed_hat * jnp.mean(grad_hat * normed_hat, axis=-1, keepdims=True)
    )


def gelu_tanh(values):
    return jax.nn.gelu(values, approximate=True)


def heads_of(values):
    return values.reshape(values.shape[0], HEADS, HEAD_DIM)


def scores_of(query_rows, key_rows, query_ids, key_ids):
    raw_scores = jnp.einsum(
        "qhe,khe->hqk", heads_of(query_rows), heads_of(key_rows), preferred_element_type=jnp.float32
    ) * HEAD_DIM ** (-0.5)
    allowed = query_ids[:, None] == key_ids[None, :]
    return jnp.where(allowed[None], raw_scores, MASKED)


def attend_row(pieces):
    query_rows, key_rows, value_rows, query_ids, key_ids = pieces
    scores = scores_of(query_rows, key_rows, query_ids, key_ids)
    row_top = jnp.max(scores, axis=-1, keepdims=True)
    exponent = jnp.exp(scores - row_top)
    row_total = jnp.sum(exponent, axis=-1, keepdims=True)
    probability = (exponent / row_total).astype(jnp.bfloat16)
    attended = jnp.einsum(
        "hqk,khe->qhe", probability, heads_of(value_rows), preferred_element_type=jnp.float32
    )
    return (
        attended.reshape(query_rows.shape[0], -1).astype(jnp.bfloat16),
        (row_top + jnp.log(row_total))[..., 0],
    )


def attend_back(pieces):
    query_rows, key_rows, value_rows, query_ids, key_ids, logsum, grad_rows = pieces
    scores = scores_of(query_rows, key_rows, query_ids, key_ids)
    probability = jnp.exp(scores - logsum[..., None])
    grad_heads = heads_of(grad_rows)
    grad_value = jnp.einsum(
        "hqk,qhe->khe",
        probability.astype(jnp.bfloat16),
        grad_heads,
        preferred_element_type=jnp.float32,
    )
    grad_probs = jnp.einsum(
        "qhe,khe->hqk", grad_heads, heads_of(value_rows), preferred_element_type=jnp.float32
    )
    centre = jnp.sum(probability * grad_probs, axis=-1, keepdims=True)
    grad_scores = (probability * (grad_probs - centre)).astype(jnp.bfloat16)
    score_scale = HEAD_DIM ** (-0.5)
    grad_query = (
        jnp.einsum(
            "hqk,khe->qhe", grad_scores, heads_of(key_rows), preferred_element_type=jnp.float32
        )
        * score_scale
    )
    grad_key = (
        jnp.einsum(
            "hqk,qhe->khe", grad_scores, heads_of(query_rows), preferred_element_type=jnp.float32
        )
        * score_scale
    )
    query_count = query_rows.shape[0]
    key_count = key_rows.shape[0]
    return (
        grad_query.reshape(query_count, -1).astype(jnp.bfloat16),
        grad_key.reshape(key_count, -1),
        grad_value.reshape(key_count, -1),
    )


def per_device(
    activations,
    out_grad,
    picture_ids,
    ln1_gain,
    ln1_bias,
    w_query,
    q_bias,
    w_key,
    w_value,
    v_bias,
    w_out,
    out_bias,
    ln2_gain,
    ln2_bias,
    w_fc1,
    fc1_bias,
    w_fc2,
    fc2_bias,
):
    row_block, local_len, width = activations.shape
    row_total = row_block * local_len
    offset = lax.axis_index("group") * local_len
    own_ids = lax.dynamic_slice_in_dim(picture_ids, offset, local_len, 1)
    (
        query_full,
        key_full,
        value_full,
        out_full,
        gain_one,
        shift_one,
        bias_query,
        bias_value,
        bias_out,
        gain_two,
        shift_two,
        bias_fc2,
    ) = (
        lax.all_gather(w_query.astype(jnp.bfloat16), "group", axis=1, tiled=True),
        lax.all_gather(w_key.astype(jnp.bfloat16), "group", axis=1, tiled=True),
        lax.all_gather(w_value.astype(jnp.bfloat16), "group", axis=1, tiled=True),
        lax.all_gather(w_out.astype(jnp.bfloat16), "group", axis=0, tiled=True),
        lax.all_gather(ln1_gain.astype(jnp.bfloat16), "group", axis=0, tiled=True),
        lax.all_gather(ln1_bias.astype(jnp.bfloat16), "group", axis=0, tiled=True),
        lax.all_gather(q_bias.astype(jnp.bfloat16), "group", axis=0, tiled=True),
        lax.all_gather(v_bias.astype(jnp.bfloat16), "group", axis=0, tiled=True),
        lax.all_gather(out_bias.astype(jnp.bfloat16), "group", axis=0, tiled=True),
        lax.all_gather(ln2_gain.astype(jnp.bfloat16), "group", axis=0, tiled=True),
        lax.all_gather(ln2_bias.astype(jnp.bfloat16), "group", axis=0, tiled=True),
        lax.all_gather(fc2_bias.astype(jnp.bfloat16), "group", axis=0, tiled=True),
    )
    inputs = activations.reshape(row_total, width)
    hat_one, inverse_one = normalize(inputs)
    normed_one = (hat_one * to_float(gain_one) + to_float(shift_one)).astype(jnp.bfloat16)
    queries = (
        jnp.dot(normed_one, query_full, preferred_element_type=jnp.float32) + to_float(bias_query)
    ).astype(jnp.bfloat16)
    keys_new = jnp.dot(normed_one, key_full, preferred_element_type=jnp.float32).astype(
        jnp.bfloat16
    )
    values_new = (
        jnp.dot(normed_one, value_full, preferred_element_type=jnp.float32) + to_float(bias_value)
    ).astype(jnp.bfloat16)
    key_all, value_all = (
        lax.all_gather(keys_new.reshape(row_block, local_len, width), "group", axis=1, tiled=True),
        lax.all_gather(
            values_new.reshape(row_block, local_len, width), "group", axis=1, tiled=True
        ),
    )
    query_rows = queries.reshape(row_block, local_len, width)
    attended, logsum = lax.map(attend_row, (query_rows, key_all, value_all, own_ids, picture_ids))
    attended = attended.reshape(row_total, width)
    middle = inputs + (
        jnp.dot(attended, out_full, preferred_element_type=jnp.float32) + to_float(bias_out)
    )
    hat_two, inverse_two = normalize(middle)
    normed_two = (hat_two * to_float(gain_two) + to_float(shift_two)).astype(jnp.bfloat16)
    fc1_full, fc2_full, bias_fc1 = (
        lax.all_gather(w_fc1.astype(jnp.bfloat16), "group", axis=1, tiled=True),
        lax.all_gather(w_fc2.astype(jnp.bfloat16), "group", axis=0, tiled=True),
        lax.all_gather(fc1_bias.astype(jnp.bfloat16), "group", axis=0, tiled=True),
    )
    hidden = jnp.dot(normed_two, fc1_full, preferred_element_type=jnp.float32) + to_float(bias_fc1)
    gelu_value, gelu_pull = jax.vjp(gelu_tanh, hidden)
    activated = gelu_value.astype(jnp.bfloat16)
    mlp_output = jnp.dot(activated, fc2_full, preferred_element_type=jnp.float32)
    output = middle + (mlp_output + to_float(bias_fc2))
    valid_rows = (own_ids >= 0).astype(jnp.float32).reshape(row_total, 1)
    grad_out = out_grad.reshape(row_total, width) * valid_rows
    grad_mlp = grad_out.astype(jnp.bfloat16)
    grad_bias_fc2 = jnp.sum(to_float(grad_mlp), axis=0)
    grad_activated = jnp.dot(grad_mlp, fc2_full.T, preferred_element_type=jnp.float32)
    grad_fc2 = jnp.dot(activated.T, grad_mlp, preferred_element_type=jnp.float32)
    grad_hidden = gelu_pull(grad_activated)[0].astype(jnp.bfloat16)
    grad_fc1 = jnp.dot(normed_two.T, grad_hidden, preferred_element_type=jnp.float32)
    grad_bias_fc1 = jnp.sum(to_float(grad_hidden), axis=0)
    grad_normed_two = jnp.dot(grad_hidden, fc1_full.T, preferred_element_type=jnp.float32)
    grad_fc1, grad_fc2, grad_bias_fc1 = (
        lax.psum_scatter(
            grad_fc1.astype(jnp.bfloat16), "group", scatter_dimension=1, tiled=True
        ).astype(jnp.float32),
        lax.psum_scatter(
            grad_fc2.astype(jnp.bfloat16), "group", scatter_dimension=0, tiled=True
        ).astype(jnp.float32),
        lax.psum_scatter(
            grad_bias_fc1.astype(jnp.bfloat16), "group", scatter_dimension=0, tiled=True
        ).astype(jnp.float32),
    )
    grad_gain_two = jnp.sum(grad_normed_two * hat_two, axis=0)
    grad_shift_two = jnp.sum(grad_normed_two, axis=0)
    grad_middle = grad_out + norm_back(grad_normed_two * to_float(gain_two), hat_two, inverse_two)
    grad_branch = grad_middle.astype(jnp.bfloat16)
    grad_bias_out = jnp.sum(to_float(grad_branch), axis=0)
    grad_out_full = jnp.dot(attended.T, grad_branch, preferred_element_type=jnp.float32)
    grad_attended = jnp.dot(grad_branch, out_full.T, preferred_element_type=jnp.float32).astype(
        jnp.bfloat16
    )
    grad_att_rows = grad_attended.reshape(row_block, local_len, width)
    grad_queries, key_parts, value_parts = lax.map(
        attend_back, (query_rows, key_all, value_all, own_ids, picture_ids, logsum, grad_att_rows)
    )
    grad_keys, grad_values = (
        lax.psum_scatter(
            key_parts.astype(jnp.bfloat16), "group", scatter_dimension=1, tiled=True
        ).astype(jnp.float32),
        lax.psum_scatter(
            value_parts.astype(jnp.bfloat16), "group", scatter_dimension=1, tiled=True
        ).astype(jnp.float32),
    )
    grad_queries = grad_queries.reshape(row_total, width)
    grad_keys = grad_keys.reshape(row_total, width).astype(jnp.bfloat16)
    grad_values = grad_values.reshape(row_total, width).astype(jnp.bfloat16)
    grad_query_full = jnp.dot(normed_one.T, grad_queries, preferred_element_type=jnp.float32)
    grad_key_full = jnp.dot(normed_one.T, grad_keys, preferred_element_type=jnp.float32)
    grad_value_full = jnp.dot(normed_one.T, grad_values, preferred_element_type=jnp.float32)
    grad_bias_query = jnp.sum(to_float(grad_queries), axis=0)
    grad_bias_value = jnp.sum(to_float(grad_values), axis=0)
    grad_normed_one = jnp.dot(grad_queries, query_full.T, preferred_element_type=jnp.float32)
    grad_normed_one = grad_normed_one + jnp.dot(
        grad_keys, key_full.T, preferred_element_type=jnp.float32
    )
    grad_normed_one = grad_normed_one + jnp.dot(
        grad_values, value_full.T, preferred_element_type=jnp.float32
    )
    grad_gain_one = jnp.sum(grad_normed_one * hat_one, axis=0)
    grad_shift_one = jnp.sum(grad_normed_one, axis=0)
    grad_input = grad_middle + norm_back(grad_normed_one * to_float(gain_one), hat_one, inverse_one)
    (
        grad_query_full,
        grad_key_full,
        grad_value_full,
        grad_out_full,
        grad_gain_one,
        grad_shift_one,
        grad_bias_query,
        grad_bias_value,
        grad_bias_out,
        grad_gain_two,
        grad_shift_two,
        grad_bias_fc2,
    ) = (
        lax.psum_scatter(
            grad_query_full.astype(jnp.bfloat16), "group", scatter_dimension=1, tiled=True
        ).astype(jnp.float32),
        lax.psum_scatter(
            grad_key_full.astype(jnp.bfloat16), "group", scatter_dimension=1, tiled=True
        ).astype(jnp.float32),
        lax.psum_scatter(
            grad_value_full.astype(jnp.bfloat16), "group", scatter_dimension=1, tiled=True
        ).astype(jnp.float32),
        lax.psum_scatter(
            grad_out_full.astype(jnp.bfloat16), "group", scatter_dimension=0, tiled=True
        ).astype(jnp.float32),
        lax.psum_scatter(
            grad_gain_one.astype(jnp.bfloat16), "group", scatter_dimension=0, tiled=True
        ).astype(jnp.float32),
        lax.psum_scatter(
            grad_shift_one.astype(jnp.bfloat16), "group", scatter_dimension=0, tiled=True
        ).astype(jnp.float32),
        lax.psum_scatter(
            grad_bias_query.astype(jnp.bfloat16), "group", scatter_dimension=0, tiled=True
        ).astype(jnp.float32),
        lax.psum_scatter(
            grad_bias_value.astype(jnp.bfloat16), "group", scatter_dimension=0, tiled=True
        ).astype(jnp.float32),
        lax.psum_scatter(
            grad_bias_out.astype(jnp.bfloat16), "group", scatter_dimension=0, tiled=True
        ).astype(jnp.float32),
        lax.psum_scatter(
            grad_gain_two.astype(jnp.bfloat16), "group", scatter_dimension=0, tiled=True
        ).astype(jnp.float32),
        lax.psum_scatter(
            grad_shift_two.astype(jnp.bfloat16), "group", scatter_dimension=0, tiled=True
        ).astype(jnp.float32),
        lax.psum_scatter(
            grad_bias_fc2.astype(jnp.bfloat16), "group", scatter_dimension=0, tiled=True
        ).astype(jnp.float32),
    )
    (
        grad_query_full,
        grad_key_full,
        grad_value_full,
        grad_out_full,
        grad_gain_one,
        grad_shift_one,
        grad_bias_query,
        grad_bias_value,
        grad_bias_out,
        grad_gain_two,
        grad_shift_two,
        grad_bias_fc2,
        grad_fc1,
        grad_fc2,
        grad_bias_fc1,
    ) = lax.psum(
        (
            grad_query_full,
            grad_key_full,
            grad_value_full,
            grad_out_full,
            grad_gain_one,
            grad_shift_one,
            grad_bias_query,
            grad_bias_value,
            grad_bias_out,
            grad_gain_two,
            grad_shift_two,
            grad_bias_fc2,
            grad_fc1,
            grad_fc2,
            grad_bias_fc1,
        ),
        "replica",
    )
    return (
        output.reshape(row_block, local_len, width),
        grad_input.reshape(row_block, local_len, width),
        grad_gain_one,
        grad_shift_one,
        grad_query_full,
        grad_bias_query,
        grad_key_full,
        grad_value_full,
        grad_bias_value,
        grad_out_full,
        grad_bias_out,
        grad_gain_two,
        grad_shift_two,
        grad_fc1,
        grad_bias_fc1,
        grad_fc2,
        grad_bias_fc2,
    )


def solution(mesh):
    placed = (
        P("replica", "group", None),
        P("replica", "group", None),
        P("replica", None),
        P("group"),
        P("group"),
        P(None, "group"),
        P("group"),
        P(None, "group"),
        P(None, "group"),
        P("group"),
        P("group", None),
        P("group"),
        P("group"),
        P("group"),
        P(None, "group"),
        P("group"),
        P("group", None),
        P("group"),
    )
    return jax.shard_map(
        per_device,
        mesh=mesh,
        in_specs=placed,
        out_specs=(
            P("replica", "group", None),
            P("replica", "group", None),
            P("group"),
            P("group"),
            P(None, "group"),
            P("group"),
            P(None, "group"),
            P(None, "group"),
            P("group"),
            P("group", None),
            P("group"),
            P("group"),
            P("group"),
            P(None, "group"),
            P("group"),
            P("group", None),
            P("group"),
        ),
        check_vma=False,
    )
```

profile of v0, /device:TPU:0, one launch (start us, length us, event | category | flops | bytes accessed | tf_op | source)
XLA Modules:
  0.0 935.0 jit_solution(2342156140588591705)
XLA Ops:
  13.8 13.2 %all-reduce.19 = (bf16[768]{0:T(1024)(128)(2,1)S(1)}, bf16[768]{0:T(1024)(128)(2,1)S(1)}, bf16[768]{0:T(1024)(128)(2,1)S(1)}, bf16[768]{0:T(1024)(128)(2,1)S(1)}...) all-reduce(bf16[768]{0:T(1024)(128)(2,1)S(1)} %dynamic-update-slice, ...), channel_id=1, replica_groups=mesh['group'=4,'replica'=8] {'group'}, use_global_device_ids=true, to_apply=%add.1 | all-reduce | flops 5376 | bytes 21504
  33.9 16.3 %all-gather.16.cloned.1.call-done = bf16[768,768]{0,1:T(8,128)(2,1)} async-done(((bf16[768,192]{0,1:T(8,128)(2,1)}), bf16[768,768]{0,1:T(8,128)(2,1)}) %all-gather.16.cloned.1.call-update) | async-done | bytes 1179664 | tf_op jit(solution)/shard_map/all_gather | solution.py:141
  72.5 28.4 %all-gather.12.cloned.1.call-done = bf16[2,1024,768]{1,2,0:T(8,128)(2,1)} async-done(((bf16[2,256,768]{1,2,0:T(8,128)(2,1)}), bf16[2,1024,768]{1,2,0:T(8,128)(2,1)}) %all-gather.12.cloned.1.call-update) | async-done | bytes 3145744 | tf_op jit(solution)/shard_map/all_gather | solution.py:167
  100.9 30.4 %all-gather.18.cloned.1.call-done = bf16[2,1024,768]{1,2,0:T(8,128)(2,1)} async-done(((bf16[2,256,768]{1,2,0:T(8,128)(2,1)}), bf16[2,1024,768]{1,2,0:T(8,128)(2,1)}) %all-gather.18.cloned.1.call-update) | async-done | bytes 3145744 | tf_op jit(solution)/shard_map/all_gather | solution.py:166
  131.2 29.5 %while.26 = (s32[]{:T(128)}, bf16[2,256,768]{2,1,0:T(8,128)(2,1)}, f32[2,12,256]{2,1,0:T(8,128)}, bf16[2,1024,768]{1,2,0:T(8,128)(2,1)}, s32[2,256]{1,0:T(2,128)...) while((s32[]{:T(128)}, bf16[2,256,768]{2,1,0:T(8,128)(2,1)}, ...), condition=%wide.region_5.6_spmd, body=%wide.region_2.5_spmd.sunk | while | flops 843510784 | bytes 51499116 | solution.py:172
  164.8 25.6 %all-gather.22.cloned.1.call-done = bf16[768,3072]{1,0:T(8,128)(2,1)} async-done(((bf16[768,768]{1,0:T(8,128)(2,1)}), bf16[768,3072]{1,0:T(8,128)(2,1)}) %all-gather.22.cloned.1.call-update) | async-done | bytes 4718608 | tf_op jit(solution)/shard_map/all_gather | solution.py:180
  190.4 8.2 fusion.28
  198.6 31.4 %all-gather.24.cloned.1.call-done = bf16[3072,768]{1,0:T(8,128)(2,1)} async-done(((bf16[768,768]{1,0:T(8,128)(2,1)}), bf16[3072,768]{1,0:T(8,128)(2,1)}) %all-gather.24.cloned.1.call-update) | async-done | bytes 4718608 | tf_op jit(solution)/shard_map/all_gather | solution.py:181
  230.0 9.8 %fusion.29 = (bf16[3072]{0:T(1024)(128)(2,1)}, bf16[512,3072]{1,0:T(8,128)(2,1)S(1)}) fusion(f32[512,3072]{1,0:T(8,128)} %fusion.28, f32[3072]{0:T(1024)S(1)} %bitcast.212, bf16[512,768]{1,0:T(8,128)(2,1)S(1)} %copy-done.22, bf16[3072,768]{1,0:T(8,128)(2,1)} %all-gather.24.cloned.1.call-done), kind=kOutput, calls=%fused_computation.108 | convolution fusion | flops 2450519040 | bytes 14960640 | tf_op jit(solution)/shard_map/dot_general | solution.py:193
  245.7 109.7 %while.27 = (s32[]{:T(128)}, bf16[2,256,768]{1,2,0:T(8,128)(2,1)}, bf16[2,1024,768]{2,1,0:T(8,128)(2,1)}, bf16[2,1024,768]{2,1,0:T(8,128)(2,1)}, bf16[2,1024,768...) while((s32[]{:T(128)}, bf16[2,256,768]{1,2,0:T(8,128)(2,1)}, ...), condition=%wide.region_12.13_spmd, body=%wide.region_10.12_spmd.sunk | while | flops 2062676992 | bytes 238015056 | solution.py:220
  258.3 11.5 %multiply_reduce_fusion.10 = (f32[12,256]{1,0:T(8,128)S(1)}, f32[12,256,1024]{2,1,0:T(8,128)}) fusion(f32[12,256,1024]{2,1,0:T(8,128)} %fusion.113, f32[12,256]{1,0:T(8,128)S(1)} %dynamic-slice_bitcast_fusion.2, pred[256,1024]{1,0:T(8,128)(4,1)S(1)} %broadcast_compare_fusion.5, bf16[256,12,64]{0,2,1:T(8,128)(2,1)S(1)} %bitcast.188, ...), kind=kOutput, calls=%fused_computation.18.clone.1 | convolution fusion | flops 418378752 | bytes 27418624 | tf_op jit(solution)/shard_map/while/body/eval_jaxpr/qhe,khe->hqk/dot_general | solution.py:75
  281.8 9.0 fusion.115
  313.0 11.5 %multiply_reduce_fusion.10 = (f32[12,256]{1,0:T(8,128)S(1)}, f32[12,256,1024]{2,1,0:T(8,128)}) fusion(f32[12,256,1024]{2,1,0:T(8,128)} %fusion.113, f32[12,256]{1,0:T(8,128)S(1)} %dynamic-slice_bitcast_fusion.2, pred[256,1024]{1,0:T(8,128)(4,1)S(1)} %broadcast_compare_fusion.5, bf16[256,12,64]{0,2,1:T(8,128)(2,1)S(1)} %bitcast.188, ...), kind=kOutput, calls=%fused_computation.18.clone.1 | convolution fusion | flops 418378752 | bytes 27418624 | tf_op jit(solution)/shard_map/while/body/eval_jaxpr/qhe,khe->hqk/dot_general | solution.py:75
  336.5 9.0 fusion.115
  364.4 29.1 %reduce-scatter.9.cloned.1.call-done = bf16[2,256,768]{2,1,0:T(8,128)(2,1)} async-done(((bf16[2,1024,768]{2,1,0:T(8,128)(2,1)}), bf16[2,256,768]{2,1,0:T(8,128)(2,1)}) %reduce-scatter.9.cloned.1.call-update) | async-done | bytes 786448 | tf_op jit(solution)/shard_map/reduce_scatter | solution.py:224
  396.9 37.2 %reduce-scatter.11.cloned.1.call-done = bf16[2,256,768]{2,1,0:T(8,128)(2,1)} async-done(((bf16[2,1024,768]{2,1,0:T(8,128)(2,1)}), bf16[2,256,768]{2,1,0:T(8,128)(2,1)}) %reduce-scatter.11.cloned.1.call-update) | async-done | bytes 786448 | tf_op jit(solution)/shard_map/reduce_scatter | solution.py:227
  445.6 8.9 convolution_convert_fusion
  465.4 26.0 %reduce-scatter.19.cloned.1.call-done = bf16[192,768]{1,0:T(8,128)(2,1)} async-done(((bf16[768,768]{1,0:T(8,128)(2,1)}), bf16[192,768]{1,0:T(8,128)(2,1)}) %reduce-scatter.19.cloned.1.call-update) | async-done | bytes 294928 | tf_op jit(solution)/shard_map/reduce_scatter | solution.py:272
  497.7 10.3 %all-reduce.18 = (bf16[768]{0:T(1024)(128)(2,1)S(1)}, bf16[768]{0:T(1024)(128)(2,1)S(1)}, bf16[768]{0:T(1024)(128)(2,1)S(1)}, bf16[768]{0:T(1024)(128)(2,1)S(1)}...) all-reduce(bf16[768]{0:T(1024)(128)(2,1)S(1)} %dynamic-update-slice, ...), channel_id=1, replica_groups=mesh['group'=4,'replica'=8] {'group'}, use_global_device_ids=true, to_apply=%add.7 | all-reduce | flops 9984 | bytes 39936
  511.8 9.3 add_add_fusion.1
  521.1 27.5 %reduce-scatter.17.cloned.1.call-done = bf16[768,192]{0,1:T(8,128)(2,1)} async-done(((bf16[768,768]{0,1:T(8,128)(2,1)}), bf16[768,192]{0,1:T(8,128)(2,1)}) %reduce-scatter.17.cloned.1.call-update) | async-done | bytes 294928 | tf_op jit(solution)/shard_map/reduce_scatter | solution.py:269
  548.6 50.2 %reduce-scatter.21.cloned.1.call-done = bf16[768,768]{1,0:T(8,128)(2,1)} async-done(((bf16[768,3072]{1,0:T(8,128)(2,1)}), bf16[768,768]{1,0:T(8,128)(2,1)}) %reduce-scatter.21.cloned.1.call-update) | async-done | bytes 1179664 | tf_op jit(solution)/shard_map/reduce_scatter | solution.py:200
  598.8 50.5 %reduce-scatter.23.cloned.1.call-done = bf16[768,768]{1,0:T(8,128)(2,1)} async-done(((bf16[3072,768]{1,0:T(8,128)(2,1)}), bf16[768,768]{1,0:T(8,128)(2,1)}) %reduce-scatter.23.cloned.1.call-update) | async-done | bytes 1179664 | tf_op jit(solution)/shard_map/reduce_scatter | solution.py:203
  649.3 279.1 %all-reduce.21 = (f32[192]{0:T(256)}, f32[192]{0:T(256)}, f32[768,192]{0,1:T(8,128)}, f32[192]{0:T(256)}, f32[768,192]{0,1:T(8,128)}, /*index=5*/f32[768,192]{0,...) all-reduce(f32[192]{0:T(256)S(1)} %dynamic-slice_convert_fusion.8, ...), channel_id=1, replica_groups=mesh['group'=4,'replica'=8] {'replica'}, use_global_device_ids=true, to_apply=%region_19.20 | all-reduce | flops 1771776 | bytes 10635264 | tf_op jit(solution)/shard_map/psum | solution.py:316
  (375 shorter events, 184.9 us)
Async XLA Ops:
  7.3 23.3 %all-gather.10.cloned.1.call-start = ((), (), s32[]{:S(2)}) async-start(), calls=%async_computation.8 | async-start | bytes 1474560 | tf_op jit(solution)/shard_map/all_gather | solution.py:142
  9.2 41.0 %all-gather.16.cloned.1.call-start = ((), (), s32[]{:S(2)}) async-start(), calls=%async_computation.11 | async-start | bytes 1474560 | tf_op jit(solution)/shard_map/all_gather | solution.py:141
  10.1 59.8 %all-gather.14.cloned.1.call-start = ((), (), s32[]{:S(2)}) async-start(), calls=%async_computation.10 | async-start | bytes 1474560 | tf_op jit(solution)/shard_map/all_gather | solution.py:140
  10.9 90.0 %all-gather.12.cloned.1.call-start = ((), (), s32[]{:S(2)}) async-start(), calls=%async_computation.9 | async-start | bytes 3932160 | tf_op jit(solution)/shard_map/all_gather | solution.py:167
  33.8 97.4 %all-gather.18.cloned.1.call-start = ((), (), s32[]{:S(2)}) async-start(), calls=%async_computation.12 | async-start | bytes 3932160 | tf_op jit(solution)/shard_map/all_gather | solution.py:166
  53.5 107.2 %all-gather.20.cloned.1.call-start = ((), (), s32[]{:S(2)}) async-start(), calls=%async_computation.13 | async-start | bytes 1474560 | tf_op jit(solution)/shard_map/all_gather | solution.py:143
  54.3 136.0 %all-gather.22.cloned.1.call-start = ((), (), s32[]{:S(2)}) async-start(), calls=%async_computation.14 | async-start | bytes 5898240 | tf_op jit(solution)/shard_map/all_gather | solution.py:180
  57.2 172.7 %all-gather.24.cloned.1.call-start = ((), (), s32[]{:S(2)}) async-start(), calls=%async_computation.15 | async-start | bytes 5898240 | tf_op jit(solution)/shard_map/all_gather | solution.py:181
  60.3 333.3 %reduce-scatter.9.cloned.1.call-start = ((), (), s32[]{:S(2)}) async-start(), calls=%async_computation.16 | async-start | bytes 3932160 | tf_op jit(solution)/shard_map/reduce_scatter | solution.py:224
  61.0 182.3 %copy-start.46 = (f32[768]{0:T(1024)}, f32[768]{0:T(1024)S(1)}, u32[]{:S(2)}) copy-start(f32[768]{0:T(1024)S(1)} %convert_element_type.279) | copy-start | bytes 9220
  61.0 129.4 %copy-start.57 = (f32[768]{0:T(1024)}, f32[768]{0:T(1024)S(1)}, u32[]{:S(2)}) copy-start(f32[768]{0:T(1024)S(1)} %convert_element_type.281) | copy-start | bytes 9220
  163.3 80.0 %copy-start.42 = (f32[512]{0:T(512)}, f32[512]{0:T(512)S(1)}, u32[]{:S(2)}) copy-start(f32[512]{0:T(512)S(1)} %broadcast_multiply_fusion.4) | copy-start | bytes 6148
  164.8 78.5 %copy-start.53 = (f32[512]{0:T(512)}, f32[512]{0:T(512)S(1)}, u32[]{:S(2)}) copy-start(f32[512]{0:T(512)S(1)} %add_rsqrt_fusion) | copy-start | bytes 6148
  164.8 65.2 %copy-start.22 = (bf16[512,768]{1,0:T(8,128)(2,1)S(1)}, bf16[512,768]{1,0:T(8,128)(2,1)}, u32[]{:S(2)}) copy-start(bf16[512,768]{1,0:T(8,128)(2,1)} %fusion.21) | copy-start | bytes 2359300
  164.8 65.2 %copy-start.48 = (f32[4,1,768]{2,1,0:T(1,128)S(1)}, f32[4,1,768]{2,1,0:T(1,128)}, u32[]{:S(2)}) copy-start(f32[4,1,768]{2,1,0:T(1,128)} %convert_element_type.326) | copy-start | bytes 36868
  355.4 78.6 %reduce-scatter.11.cloned.1.call-start = ((), (), s32[]{:S(2)}) async-start(), calls=%async_computation.17 | async-start | bytes 3932160 | tf_op jit(solution)/shard_map/reduce_scatter | solution.py:227
  356.0 109.3 %reduce-scatter.13.cloned.1.call-start = ((), (), s32[]{:S(2)}) async-start(), calls=%async_computation.18 | async-start | bytes 1474560 | tf_op jit(solution)/shard_map/reduce_scatter | solution.py:263
  361.4 130.0 %reduce-scatter.19.cloned.1.call-start = ((), (), s32[]{:S(2)}) async-start(), calls=%async_computation.21 | async-start | bytes 1474560 | tf_op jit(solution)/shard_map/reduce_scatter | solution.py:272
  364.4 156.7 %reduce-scatter.15.cloned.1.call-start = ((), (), s32[]{:S(2)}) async-start(), calls=%async_computation.19 | async-start | bytes 1474560 | tf_op jit(solution)/shard_map/reduce_scatter | solution.py:266
  396.8 151.8 %reduce-scatter.17.cloned.1.call-start = ((), (), s32[]{:S(2)}) async-start(), calls=%async_computation.20 | async-start | bytes 1474560 | tf_op jit(solution)/shard_map/reduce_scatter | solution.py:269
  437.4 161.5 %reduce-scatter.21.cloned.1.call-start = ((), (), s32[]{:S(2)}) async-start(), calls=%async_computation.22 | async-start | bytes 5898240 | tf_op jit(solution)/shard_map/reduce_scatter | solution.py:200
  444.9 204.4 %reduce-scatter.23.cloned.1.call-start = ((), (), s32[]{:S(2)}) async-start(), calls=%async_computation.23 | async-start | bytes 5898240 | tf_op jit(solution)/shard_map/reduce_scatter | solution.py:203
  511.8 137.5 %copy-start.28 = (bf16[768,192]{0,1:T(8,128)(2,1)S(1)}, bf16[768,192]{0,1:T(8,128)(2,1)}, u32[]{:S(2)}) copy-start(bf16[768,192]{0,1:T(8,128)(2,1)} %reduce-scatter.13.cloned.1.call-done) | copy-start | bytes 884740
  511.8 137.5 %copy-start.29 = (bf16[192,768]{1,0:T(8,128)(2,1)S(1)}, bf16[192,768]{1,0:T(8,128)(2,1)}, u32[]{:S(2)}) copy-start(bf16[192,768]{1,0:T(8,128)(2,1)} %reduce-scatter.19.cloned.1.call-done) | copy-start | bytes 884740
  (83 other events, 523.9 us)
Sparse Core Ops, SparseCore 0:
  10.3 20.2 all-gather.9
  32.7 17.4 all-gather.15
  52.3 17.5 all-gather.13
  71.9 28.9 all-gather.11
  102.2 28.9 all-gather.17
  133.2 17.4 all-gather.19
  152.8 37.4 all-gather.21
  192.5 37.4 all-gather.23
  355.6 37.9 reduce-scatter.8
  396.1 37.9 reduce-scatter.10
  437.2 25.7 reduce-scatter.12
  465.6 25.7 reduce-scatter.18
  494.5 25.7 reduce-scatter.14
  522.8 25.7 reduce-scatter.16
  551.0 47.8 reduce-scatter.20
  601.4 47.8 reduce-scatter.22
where the time goes:
time: 942 us; the launch traced here: 935 us
  waiting for transfers between devices  356 us (38%)
  blocking collectives  308 us (33%)
  matrix products  151 us (16%)
  local copies, waits for them, and re-layouts  54.9 us (6%)
  other arithmetic  47.5 us (5%)
  between operations  17 us (2%)
    psum x1, blocking collectives, per_device(): lax.psum((grad_query_full, grad_key_full, grad_value_full, grad_out_full,...  279 us
    reduce_scatter x1, waiting for transfers between devices, per_device(): lax.psum_scatter(grad_fc2.astype(jnp.bfloat16), 'group', scatter_dimensio...  50.5 us
    reduce_scatter x1, waiting for transfers between devices, per_device(): lax.psum_scatter(grad_fc1.astype(jnp.bfloat16), 'group', scatter_dimensio...  50.2 us
    reduce_scatter x1, waiting for transfers between devices, per_device(): lax.psum_scatter(value_parts.astype(jnp.bfloat16), 'group', scatter_dimen...  37.2 us
    all_gather x1, waiting for transfers between devices, per_device(): lax.all_gather(w_fc2.astype(jnp.bfloat16), 'group', axis=0, tiled=True)  31.4 us
    all_gather x1, waiting for transfers between devices, per_device(): lax.all_gather(keys_new.reshape(row_block, local_len, width), 'group', ax...  30.4 us
    reduce_scatter x1, waiting for transfers between devices, per_device(): lax.psum_scatter(key_parts.astype(jnp.bfloat16), 'group', scatter_dimensi...  29.1 us
    all_gather x1, waiting for transfers between devices, per_device(): lax.all_gather(values_new.reshape(row_block, local_len, width), 'group',...  28.4 us
  transfers between devices with their start and end apart: 16, of which 13 were waited for; matrix products, arithmetic and copies ran while one was open for 13% of the time, Pallas kernels for 0%

commit v1 on v0

v1 whole, which is shorter than its diff:
```python
import jax
import jax.numpy as jnp
from jax import lax
from jax.experimental import pallas as pl
from jax.experimental.pallas import tpu as pltpu
from jax.sharding import PartitionSpec as P

HEADS = 12
HEAD_DIM = 64
EPS = 1e-06
MASKED = -1e30
BF = jnp.bfloat16
F32 = jnp.float32
PAIR = 2 * HEAD_DIM
Q_BLOCK = 256


def to_float(values):
    return values.astype(F32)


def normalize(values):
    centred = values - jnp.mean(values, axis=-1, keepdims=True)
    inverse = lax.rsqrt(jnp.mean(centred * centred, axis=-1, keepdims=True) + EPS)
    return (centred * inverse, inverse)


def norm_back(grad_hat, normed_hat, inverse):
    return inverse * (
        grad_hat
        - jnp.mean(grad_hat, axis=-1, keepdims=True)
        - normed_hat * jnp.mean(grad_hat * normed_hat, axis=-1, keepdims=True)
    )


def gelu_tanh(values):
    return jax.nn.gelu(values, approximate=True)


def dot_nn(left, right):
    return jnp.dot(left, right, preferred_element_type=F32)


def dot_nt(left, right):
    return lax.dot_general(left, right, (((1,), (1,)), ((), ())), preferred_element_type=F32)


def dot_tn(left, right):
    return lax.dot_general(left, right, (((0,), (0,)), ((), ())), preferred_element_type=F32)


def attend_kernel(q_ref, k_ref, v_ref, iq_ref, ik_ref, out_ref, prob_ref):
    first = lax.broadcasted_iota(jnp.int32, (1, PAIR), 1) < HEAD_DIM
    queries = q_ref[...] * jnp.asarray(HEAD_DIM**-0.5, BF)
    allowed = iq_ref[...] == ik_ref[...]
    parts = []
    for head in range(2):
        lanes = first if head == 0 else ~first
        scores = dot_nt(jnp.where(lanes, queries, jnp.zeros_like(queries)), k_ref[...])
        scores = jnp.where(allowed, scores, MASKED)
        exponent = jnp.exp(scores - jnp.max(scores, axis=1, keepdims=True))
        scale = 1.0 / jnp.sum(exponent, axis=1, keepdims=True)
        probability = (exponent * scale).astype(BF)
        prob_ref[head] = probability
        parts.append(dot_nn(probability, v_ref[...]))
    out_ref[...] = jnp.where(first, parts[0], parts[1]).astype(BF)


def attend(queries, keys, values, ids):
    length, width = queries.shape
    pairs = width // PAIR
    query_spec = pl.BlockSpec((Q_BLOCK, PAIR), lambda p, i: (i, p))
    key_spec = pl.BlockSpec((length, PAIR), lambda p, i: (0, p))
    return pl.pallas_call(
        attend_kernel,
        grid=(pairs, length // Q_BLOCK),
        in_specs=[
            query_spec,
            key_spec,
            key_spec,
            pl.BlockSpec((Q_BLOCK, 1), lambda p, i: (i, 0)),
            pl.BlockSpec((1, length), lambda p, i: (0, 0)),
        ],
        out_specs=[query_spec, pl.BlockSpec((2, Q_BLOCK, length), lambda p, i: (p, i, 0))],
        out_shape=[
            jax.ShapeDtypeStruct((length, width), BF),
            jax.ShapeDtypeStruct((2 * pairs, length, length), BF),
        ],
        compiler_params=pltpu.CompilerParams(vmem_limit_bytes=40 << 20),
        name="attend",
    )(queries, keys, values, ids[:, None], ids[None, :])


def attend_back_kernel(
    q_ref, k_ref, v_ref, out_ref, grad_ref, prob_ref, dq_ref, dk_ref, dv_ref, key_sum, value_sum
):
    step = pl.program_id(1)
    first = lax.broadcasted_iota(jnp.int32, (1, PAIR), 1) < HEAD_DIM
    queries, keys, grad = q_ref[...], k_ref[...], grad_ref[...]
    product = to_float(grad) * to_float(out_ref[...])

    @pl.when(step == 0)
    def _():
        key_sum[...] = jnp.zeros_like(key_sum)
        value_sum[...] = jnp.zeros_like(value_sum)

    grad_queries = None
    for head in range(2):
        lanes = first if head == 0 else ~first
        grad_head = jnp.where(lanes, grad, jnp.zeros_like(grad))
        query_head = jnp.where(lanes, queries, jnp.zeros_like(queries))
        key_head = jnp.where(lanes, keys, jnp.zeros_like(keys))
        centre = jnp.sum(jnp.where(lanes, product, 0.0), axis=1, keepdims=True)
        probability = prob_ref[head]
        grad_probs = dot_nt(grad_head, v_ref[...])
        grad_scores = (to_float(probability) * (grad_probs - centre)).astype(BF)
        part = dot_nn(grad_scores, key_head)
        grad_queries = part if head == 0 else grad_queries + part
        key_sum[...] += dot_tn(grad_scores, query_head)
        value_sum[...] += dot_tn(probability, grad_head)
    dq_ref[...] = (grad_queries * HEAD_DIM**-0.5).astype(BF)

    @pl.when(step == pl.num_programs(1) - 1)
    def _():
        dk_ref[...] = (key_sum[...] * HEAD_DIM**-0.5).astype(BF)
        dv_ref[...] = value_sum[...].astype(BF)


def attend_back(queries, keys, values, attended, grad_attended, probability):
    length, width = queries.shape
    query_spec = pl.BlockSpec((Q_BLOCK, PAIR), lambda p, i: (i, p))
    key_spec = pl.BlockSpec((length, PAIR), lambda p, i: (0, p))
    return pl.pallas_call(
        attend_back_kernel,
        grid=(width // PAIR, length // Q_BLOCK),
        in_specs=[
            query_spec,
            key_spec,
            key_spec,
            query_spec,
            query_spec,
            pl.BlockSpec((2, Q_BLOCK, length), lambda p, i: (p, i, 0)),
        ],
        out_specs=[query_spec, key_spec, key_spec],
        out_shape=[jax.ShapeDtypeStruct((length, width), BF)] * 3,
        scratch_shapes=[pltpu.VMEM((length, PAIR), F32)] * 2,
        compiler_params=pltpu.CompilerParams(vmem_limit_bytes=40 << 20),
        name="attend_back",
    )(queries, keys, values, attended, grad_attended, probability)


def swap(values, axis, size, bit):
    return lax.ppermute(values, axis, [(i, i ^ bit) for i in range(size)])


def core_swap(values):
    return swap(values, "group", 4, 1)


def chip_swap(values):
    return swap(values, "group", 4, 2)


def replica_sum(rows, size):
    index = lax.axis_index("replica")
    bits = []
    bit = 1
    while bit < size:
        bits.append(bit)
        bit *= 2
    for bit in bits:
        half = rows.shape[0] // 2
        mine = (index // bit) % 2
        sent = lax.dynamic_slice_in_dim(rows, (1 - mine) * half, half, 0)
        kept = lax.dynamic_slice_in_dim(rows, mine * half, half, 0)
        rows = (to_float(kept) + to_float(swap(sent, "replica", size, bit))).astype(BF)
    for bit in reversed(bits):
        mine = (index // bit) % 2
        other = swap(rows, "replica", size, bit)
        rows = jnp.concatenate(
            [jnp.where(mine == 0, rows, other), jnp.where(mine == 0, other, rows)], axis=0
        )
    return rows


def per_device(
    replicas,
    activations,
    out_grad,
    picture_ids,
    ln1_gain,
    ln1_bias,
    w_query,
    q_bias,
    w_key,
    w_value,
    v_bias,
    w_out,
    out_bias,
    ln2_gain,
    ln2_bias,
    w_fc1,
    fc1_bias,
    w_fc2,
    fc2_bias,
):
    row_block, quarter, width = activations.shape
    assert row_block == 2
    shard = w_query.shape[1]
    half = 2 * quarter
    group = lax.axis_index("group")
    core = group % 2

    def own_row(values):
        return lax.dynamic_index_in_dim(values, core, 0, keepdims=False)

    def other_row(values):
        return lax.dynamic_index_in_dim(values, 1 - core, 0, keepdims=False)

    def home(values):
        kept, sent = values[:quarter], values[quarter:]
        got = core_swap(sent)
        return jnp.stack([jnp.where(core == 0, kept, got), jnp.where(core == 0, got, kept)])

    small = jnp.concatenate(
        [ln1_gain, ln1_bias, out_bias, ln2_gain, ln2_bias, fc2_bias, q_bias, v_bias, fc1_bias]
    ).astype(BF)
    small_chip = chip_swap(small)
    both = jnp.stack([small, small_chip])
    both_core = core_swap(both)
    shards = [both[0], both_core[0], both[1], both_core[1]]

    def full(position):
        part = jnp.stack([s[position * shard : (position + 1) * shard] for s in shards])
        return jnp.concatenate(
            [lax.dynamic_index_in_dim(part, group ^ i, 0) for i in range(4)], axis=0
        ).reshape(-1)

    gain_one, shift_one, bias_out, gain_two, shift_two, bias_fc2 = [
        to_float(full(i)) for i in range(6)
    ]

    def pair(start, size):
        return to_float(
            jnp.concatenate([shards[0][start : start + size], shards[1][start : start + size]])
        )

    bias_query = pair(6 * shard, shard)
    bias_value = pair(7 * shard, shard)
    bias_fc1 = pair(8 * shard, fc1_bias.shape[0])

    inputs = jnp.concatenate([own_row(activations), core_swap(other_row(activations))], axis=0)
    own_ids = lax.dynamic_slice_in_dim(picture_ids, group * quarter, quarter, 1)
    grad_home = out_grad * (own_ids >= 0).astype(F32)[..., None]
    grad_out = jnp.concatenate([own_row(grad_home), core_swap(other_row(grad_home))], axis=0)
    row_ids = own_row(picture_ids).reshape(4, quarter)
    ids = jnp.concatenate(
        [lax.dynamic_index_in_dim(row_ids, group ^ i, 0, keepdims=False) for i in range(4)]
    )

    hat_one, inverse_one = normalize(inputs)
    normed_own = (hat_one * gain_one + shift_one).astype(BF)
    normed_one = jnp.concatenate([normed_own, chip_swap(normed_own)], axis=0)
    grad_mlp_own = grad_out.astype(BF)
    grad_mlp = jnp.concatenate([grad_mlp_own, chip_swap(grad_mlp_own)], axis=0)

    projections = jnp.stack([w_query, w_key, w_value]).astype(BF)
    partner = core_swap(projections)
    w_qkv = jnp.concatenate(
        [part for i in range(3) for part in (projections[i], partner[i])], axis=1
    )
    down = jnp.concatenate([w_out, w_fc2], axis=0).astype(BF)
    down_partner = core_swap(down)
    out_full = jnp.concatenate([down[:shard], down_partner[:shard]], axis=0)
    fc2_full = jnp.concatenate([down[shard:], down_partner[shard:]], axis=0)
    up = w_fc1.astype(BF)
    fc1_full = jnp.concatenate([up, core_swap(up)], axis=1)

    bias_qkv = jnp.concatenate([bias_query, jnp.zeros_like(bias_query), bias_value])
    qkv = (dot_nn(normed_one, w_qkv) + bias_qkv).astype(BF)
    span = 2 * shard
    queries, keys, values = qkv[:, :span], qkv[:, span : 2 * span], qkv[:, 2 * span :]
    attended, probability = attend(queries, keys, values, ids)
    branch = dot_nn(attended, out_full)
    branch_other = chip_swap(branch[half:].astype(BF))
    middle = inputs + (branch[:half] + to_float(branch_other) + bias_out)

    hat_two, inverse_two = normalize(middle)
    normed_two_own = (hat_two * gain_two + shift_two).astype(BF)
    normed_two = jnp.concatenate([normed_two_own, chip_swap(normed_two_own)], axis=0)
    hidden = dot_nn(normed_two, fc1_full) + bias_fc1
    gelu_value, gelu_pull = jax.vjp(gelu_tanh, hidden)
    activated = gelu_value.astype(BF)
    grad_hidden = gelu_pull(dot_nt(grad_mlp, fc2_full))[0].astype(BF)
    grad_normed = dot_nt(grad_hidden, fc1_full)
    grad_normed_other = chip_swap(grad_normed[half:].astype(BF))
    grad_normed_two = grad_normed[:half] + to_float(grad_normed_other)
    mlp = dot_nn(activated, fc2_full)
    mlp_other = chip_swap(mlp[half:].astype(BF))
    output = home(middle + (mlp[:half] + to_float(mlp_other) + bias_fc2))

    grad_middle = grad_out + norm_back(grad_normed_two * gain_two, hat_two, inverse_two)
    grad_branch_own = grad_middle.astype(BF)
    grad_branch = jnp.concatenate([grad_branch_own, chip_swap(grad_branch_own)], axis=0)

    grad_fc1 = dot_tn(normed_two, grad_hidden).astype(BF)
    grad_fc2 = dot_tn(activated, grad_mlp).astype(BF)
    wide = fc1_full.shape[1] // 2
    fc_kept = jnp.concatenate([grad_fc1[:, :wide], grad_fc2[:wide]], axis=0)
    fc_sent = jnp.concatenate([grad_fc1[:, wide:], grad_fc2[wide:]], axis=0)
    fc_rows = (to_float(fc_kept) + to_float(core_swap(fc_sent))).astype(BF)
    fc_rows = replica_sum(fc_rows, replicas)
    grad_w_fc1 = to_float(fc_rows[:width])
    grad_w_fc2 = to_float(fc_rows[width:])

    grad_attended = dot_nt(grad_branch, out_full).astype(BF)
    grad_queries, grad_keys, grad_values = attend_back(
        queries, keys, values, attended, grad_attended, probability
    )
    grad_qkv = jnp.concatenate([grad_queries, grad_keys, grad_values], axis=1)
    grad_first = dot_nt(grad_qkv, w_qkv)
    grad_first_other = chip_swap(grad_first[half:].astype(BF))
    grad_normed_one = grad_first[:half] + to_float(grad_first_other)
    grad_input = home(
        grad_middle + norm_back(grad_normed_one * gain_one, hat_one, inverse_one)
    )

    grad_w_qkv = dot_tn(grad_qkv, normed_one).astype(BF)
    grad_w_out = dot_tn(attended, grad_branch).astype(BF)

    def total(values):
        return jnp.sum(to_float(values), axis=0)

    wide_sums = jnp.stack(
        [
            jnp.sum(grad_normed_one * hat_one, axis=0),
            jnp.sum(grad_normed_one, axis=0),
            total(grad_branch_own),
            jnp.sum(grad_normed_two * hat_two, axis=0),
            jnp.sum(grad_normed_two, axis=0),
            total(grad_mlp_own),
        ]
    ).astype(BF)
    by_shard = jnp.transpose(wide_sums.reshape(6, 4, shard), (1, 0, 2))

    def shard_of(i):
        return lax.dynamic_index_in_dim(by_shard, group ^ i, 0, keepdims=False)

    chip_part = chip_swap(jnp.stack([shard_of(2), shard_of(3)]))
    small_own = to_float(shard_of(0)) + to_float(chip_part[0])
    small_core = to_float(shard_of(1)) + to_float(chip_part[1])
    bias_sums = total(grad_queries), total(grad_values), total(grad_hidden)

    def side(index):
        return [
            s[index * (s.shape[0] // 2) : (index + 1) * (s.shape[0] // 2)] for s in bias_sums
        ]

    kept_small = jnp.concatenate([small_own.reshape(-1)] + side(0))
    sent_small = jnp.concatenate([small_core.reshape(-1)] + side(1)).astype(BF)
    small_rows = kept_small.shape[0] // width
    padding = -small_rows % replicas

    def padded(values):
        return jnp.pad(values.reshape(small_rows, width), ((0, padding), (0, 0)))

    def arranged(index, vector):
        rows = [grad_w_out[index * shard : (index + 1) * shard]]
        for i in range(3):
            start = i * span + index * shard
            rows.append(grad_w_qkv[start : start + shard])
        rows.append(padded(vector).astype(BF))
        return jnp.concatenate(rows, axis=0)

    attention_rows = (
        to_float(arranged(0, kept_small)) + to_float(core_swap(arranged(1, sent_small)))
    ).astype(BF)
    attention_rows = replica_sum(attention_rows, replicas)
    sums = to_float(attention_rows[4 * shard : 4 * shard + small_rows]).reshape(-1)

    def vector(position):
        return sums[position * shard : (position + 1) * shard]

    def weight(index):
        return to_float(attention_rows[index * shard : (index + 1) * shard])

    return (
        output,
        grad_input,
        vector(0),
        vector(1),
        weight(1).T,
        vector(6),
        weight(2).T,
        weight(3).T,
        vector(7),
        weight(0),
        vector(2),
        vector(3),
        vector(4),
        grad_w_fc1,
        sums[8 * shard :],
        grad_w_fc2,
        vector(5),
    )


def solution(mesh):
    replicas = mesh.shape["replica"]
    assert mesh.shape["group"] == 4
    patches = P("replica", "group", None)
    vector = P("group")
    columns = P(None, "group")
    rows = P("group", None)

    def program(*arguments):
        return per_device(replicas, *arguments)

    return jax.shard_map(
        program,
        mesh=mesh,
        in_specs=(
            patches,
            patches,
            P("replica", None),
            vector,
            vector,
            columns,
            vector,
            columns,
            columns,
            vector,
            rows,
            vector,
            vector,
            vector,
            columns,
            vector,
            rows,
            vector,
        ),
        out_specs=(
            patches,
            patches,
            vector,
            vector,
            columns,
            vector,
            columns,
            columns,
            vector,
            rows,
            vector,
            vector,
            vector,
            columns,
            vector,
            rows,
            vector,
        ),
        check_vma=False,
    )
```

time: 942 us -> 414 us (0.44)
  blocking collectives: 308 us -> 0 us
  waiting for transfers between devices: 356 us -> 193 us
  matrix products: 151 us -> 41 us
  Pallas kernels: 0 us -> 39.8 us
  starting transfers between devices: 0.84 us -> 26 us
  between operations: 17 us -> 2 us
    psum x1 -> x0, blocking collectives: 279 us -> none  [per_device(): lax.psum((grad_query_full, grad_key_full, grad_value_full, grad_out_full,...]
    reduce_scatter x8 -> x0, waiting for transfers between devices: 220 us -> none  [the longest x1 50.5 us: per_device(): lax.psum_scatter(grad_fc2.astype(jnp.bfloat16), 'group', scatter_dimensio...]
    ppermute x0 -> x32, waiting for transfers between devices: none -> 193 us  [swap(): return lax.ppermute(values, axis, [(i, i ^ bit) for i in range(size)])]
    all_gather x8 -> x0, waiting for transfers between devices: 135 us -> none  [the longest x1 31.4 us: per_device(): lax.all_gather(w_fc2.astype(jnp.bfloat16), 'group', axis=0, tiled=True)]
    dot_general x32 -> x12, matrix products: 151 us -> 41 us  [the longest x4 16.5 us: dot_nt(): lax.dot_general(left, right, (((1,), (1,)), ((), ())), preferred_element_...]
    pallas_call x0 -> x2, Pallas kernels: none -> 39.8 us  [the longest x1 20.8 us: attend_back(): pl.pallas_call(attend_back_kernel, grid=(width // PAIR, length // Q_BLOCK...]
    ppermute x0 -> x32, starting transfers between devices: none -> 26 us  [swap(): return lax.ppermute(values, axis, [(i, i ^ bit) for i in range(size)])]
    unnamed x2 -> x0, blocking collectives: 23.4 us -> none
  transfers between devices with their start and end apart: 16 -> 32, of which waited for: 13 -> 19; matrix products, arithmetic and copies ran while one was open for 13% -> 27% of each run, Pallas kernels for 0% -> 10%
where the time goes in v1:
time: 414 us; the launch traced here: 407 us
  waiting for transfers between devices  193 us (47%)
  other arithmetic  54.7 us (13%)
  local copies, waits for them, and re-layouts  51.2 us (12%)
  matrix products  41 us (10%)
  Pallas kernels  39.8 us (10%)
  starting transfers between devices  26 us (6%)
    ppermute x32, waiting for transfers between devices, swap(): return lax.ppermute(values, axis, [(i, i ^ bit) for i in range(size)])  193 us
    ppermute x32, starting transfers between devices, swap(): return lax.ppermute(values, axis, [(i, i ^ bit) for i in range(size)])  26 us
    pallas_call x1, Pallas kernels, attend_back(): pl.pallas_call(attend_back_kernel, grid=(width // PAIR, length // Q_BLOCK...  20.8 us
    pallas_call x1, Pallas kernels, attend(): pl.pallas_call(attend_kernel, grid=(pairs, length // Q_BLOCK), in_specs=[...  19 us
    dot_general x4, matrix products, dot_nt(): lax.dot_general(left, right, (((1,), (1,)), ((), ())), preferred_element_...  16.5 us
    unnamed x106, local copies, waits for them, and re-layouts  12.8 us
    dot_general x4, matrix products, dot_tn(): lax.dot_general(left, right, (((0,), (0,)), ((), ())), preferred_element_...  12.6 us
    dot_general x4, matrix products, dot_nn(): return jnp.dot(left, right, preferred_element_type=F32)  11.9 us
  transfers between devices with their start and end apart: 32, of which 19 were waited for; matrix products, arithmetic and copies ran while one was open for 27% of the time, Pallas kernels for 10%

profile of v1, /device:TPU:0, one launch (start us, length us, event | category | flops | bytes accessed | tf_op | source)
XLA Modules:
  0.0 407.4 jit_solution(16412208485316644086)
XLA Ops:
  33.6 14.6 %collective-permute-done.3 = bf16[512,768]{1,0:T(8,128)(2,1)S(1)} collective-permute-done((bf16[512,768]{1,0:T(8,128)(2,1)S(1)}, bf16[512,768]{1,0:T(8,128)(2,1)S(1)}, u32[]{:S(2)}, u32[]{:S(2)}) %collective-permute-start.3) | collective-permute-done | bytes 786464 | tf_op jit(solution)/shard_map/ppermute | solution.py:153
  51.5 19.0 %attend.1 = (bf16[1024,384]{1,0:T(8,128)(2,1)S(1)}, bf16[6,1024,1024]{2,1,0:T(8,128)(2,1)}) custom-call(bf16[1024,384]{1,0:T(8,128)(2,1)S(1)} %get-tuple-element.58.q_ref, bf16[1024,384]{1,0:T(8,128)(2,1)S(1)} %get-tuple-element.57.k_ref, bf16[1024,384]{1,0:T(8,128)(2,1)S(1)} %get-tuple-element.56.v_ref, s32[1024,1]{1,0:T(8,128)S(1)} %copy-done, ...), custom_call_target="tpu_custom_call" | custom-call | tf_op jit(solution)/shard_map/attend/pallas_call | solution.py:74
  74.7 18.4 %collective-permute-done.6 = bf16[512,768]{1,0:T(8,128)(2,1)} collective-permute-done((bf16[512,768]{1,0:T(8,128)(2,1)}, bf16[512,768]{1,0:T(8,128)(2,1)}, u32[]{:S(2)}, u32[]{:S(2)}) %collective-permute-start.6) | collective-permute-done | bytes 786464 | tf_op jit(solution)/shard_map/ppermute | solution.py:153
  103.7 14.2 %collective-permute-done.7 = bf16[512,768]{1,0:T(8,128)(2,1)} collective-permute-done((bf16[512,768]{1,0:T(8,128)(2,1)}, bf16[512,768]{1,0:T(8,128)(2,1)}, u32[]{:S(2)}, u32[]{:S(2)}) %collective-permute-start.7) | collective-permute-done | bytes 786464 | tf_op jit(solution)/shard_map/ppermute | solution.py:153
  117.9 4.7 %fusion.14 = f32[1024,1536]{1,0:T(8,128)S(1)} fusion(bf16[768,768]{1,0:T(8,128)(2,1)} %collective-permute-done.8, bf16[768,768]{1,0:T(8,128)(2,1)} %convert_element_type.299, bf16[512,768]{1,0:T(8,128)(2,1)} %collective-permute-done.7, bf16[512,768]{1,0:T(8,128)(2,1)} %add_convert_fusion.4), kind=kOutput, calls=%fused_computation.53 | convolution fusion | flops 2423783424 | bytes 10223616 | tf_op jit(solution)/shard_map/dot_general | solution.py:41
  122.6 4.0 fusion.12
  126.6 5.4 %collective-permute-done.12 = bf16[512,768]{1,0:T(8,128)(2,1)S(1)} collective-permute-done((bf16[512,768]{1,0:T(8,128)(2,1)}, bf16[512,768]{1,0:T(8,128)(2,1)S(1)}, u32[]{:S(2)}, u32[]{:S(2)}) %collective-permute-start.12) | collective-permute-done | bytes 786464 | tf_op jit(solution)/shard_map/ppermute | solution.py:153
  132.0 7.6 %fusion.55 = (bf16[1536]{0:T(1024)(128)(2,1)S(1)}, bf16[1024,1536]{1,0:T(8,128)(2,1)S(1)}) fusion(f32[1024,1536]{1,0:T(8,128)S(1)} %fusion.14, f32[1536]{0:T(1024)S(1)} %maximum_convert_fusion, bf16[768,768]{1,0:T(8,128)(2,1)S(1)} %slice.402, bf16[768,768]{1,0:T(8,128)(2,1)S(1)} %copy-done.16, bf16[512,768]{1,0:T(8,128)(2,1)S(1)} %collective-permute-done.12, ...), kind=kOutput, calls=%fused_computation.243 | convolution fusion | flops 2458384896 | bytes 13378560 | tf_op jit(solution)/shard_map/dot_general | solution.py:45
  139.6 4.3 %fusion.13 = f32[1024,768]{1,0:T(8,128)S(1)} fusion(bf16[1024,1536]{1,0:T(8,128)(2,1)S(1)} %get-tuple-element.157, bf16[768,768]{1,0:T(8,128)(2,1)} %collective-permute-done.8, bf16[768,768]{1,0:T(8,128)(2,1)} %convert_element_type.299), kind=kOutput, calls=%fused_computation.52 | convolution fusion | flops 2420637696 | bytes 8650752 | tf_op jit(solution)/shard_map/dot_general | solution.py:45
  151.3 4.4 %convolution_convert_fusion.1 = bf16[768,1536]{1,0:T(8,128)(2,1)S(1)} fusion(bf16[1024,1536]{1,0:T(8,128)(2,1)S(1)} %get-tuple-element.157, bf16[512,768]{1,0:T(8,128)(2,1)} %collective-permute-done.7, bf16[512,768]{1,0:T(8,128)(2,1)} %add_convert_fusion.4), kind=kOutput, calls=%fused_computation.13 | convolution fusion | flops 2420244480 | bytes 7077888 | tf_op jit(solution)/shard_map/dot_general | solution.py:49
  155.7 8.9 %collective-permute-done.9 = bf16[512,768]{1,0:T(8,128)(2,1)S(1)} collective-permute-done((bf16[512,768]{1,0:T(8,128)(2,1)S(1)}, bf16[512,768]{1,0:T(8,128)(2,1)S(1)}, u32[]{:S(2)}, u32[]{:S(2)}) %collective-permute-start.9) | collective-permute-done | bytes 786464 | tf_op jit(solution)/shard_map/ppermute | solution.py:153
  164.6 13.3 %collective-permute-done.13 = bf16[512,768]{1,0:T(8,128)(2,1)S(1)} collective-permute-done((bf16[512,768]{1,0:T(8,128)(2,1)S(1)}, bf16[512,768]{1,0:T(8,128)(2,1)S(1)}, u32[]{:S(2)}, u32[]{:S(2)}) %collective-permute-start.13) | collective-permute-done | bytes 786464 | tf_op jit(solution)/shard_map/ppermute | solution.py:153
  192.3 7.1 %collective-permute-done.14 = bf16[512,768]{1,0:T(8,128)(2,1)} collective-permute-done((bf16[512,768]{1,0:T(8,128)(2,1)}, bf16[512,768]{1,0:T(8,128)(2,1)}, u32[]{:S(2)}, u32[]{:S(2)}) %collective-permute-start.14) | collective-permute-done | bytes 786464 | tf_op jit(solution)/shard_map/ppermute | solution.py:153
  201.7 20.8 %attend_back.1 = (bf16[1024,384]{1,0:T(8,128)(2,1)S(1)}, bf16[1024,384]{1,0:T(8,128)(2,1)S(1)}, bf16[1024,384]{1,0:T(8,128)(2,1)S(1)}) custom-call(bf16[1024,384]{1,0:T(8,128)(2,1)S(1)} %get-tuple-element.58.q_ref, bf16[1024,384]{1,0:T(8,128)(2,1)S(1)} %get-tuple-element.57.k_ref, bf16[1024,384]{1,0:T(8,128)(2,1)S(1)} %get-tuple-element.56.v_ref, ...), custom_call_target="tpu_custom_call" | custom-call | tf_op jit(solution)/shard_map/attend_back/pallas_call | solution.py:133
  233.4 8.6 %collective-permute-done.15 = bf16[512,768]{1,0:T(8,128)(2,1)S(1)} collective-permute-done((bf16[512,768]{1,0:T(8,128)(2,1)S(1)}, bf16[512,768]{1,0:T(8,128)(2,1)S(1)}, u32[]{:S(2)}, u32[]{:S(2)}) %collective-permute-start.15) | collective-permute-done | bytes 786464 | tf_op jit(solution)/shard_map/ppermute | solution.py:153
  283.0 11.8 %collective-permute-done.26 = bf16[768,768]{1,0:T(8,128)(2,1)} collective-permute-done((bf16[768,768]{1,0:T(8,128)(2,1)S(1)}, bf16[768,768]{1,0:T(8,128)(2,1)}, u32[]{:S(2)}, u32[]{:S(2)}) %collective-permute-start.26) | collective-permute-done | bytes 1179680 | tf_op jit(solution)/shard_map/ppermute | solution.py:153
  297.5 9.7 %collective-permute-done.19 = bf16[388,768]{1,0:T(8,128)(2,1)S(1)} collective-permute-done((bf16[388,768]{1,0:T(8,128)(2,1)S(1)}, bf16[388,768]{1,0:T(8,128)(2,1)S(1)}, u32[]{:S(2)}, u32[]{:S(2)}) %collective-permute-start.19) | collective-permute-done | bytes 596000 | tf_op jit(solution)/shard_map/ppermute | solution.py:153
  314.5 8.7 %collective-permute-done.20 = bf16[194,768]{1,0:T(8,128)(2,1)S(1)} collective-permute-done((bf16[194,768]{1,0:T(8,128)(2,1)S(1)}, bf16[194,768]{1,0:T(8,128)(2,1)S(1)}, u32[]{:S(2)}, u32[]{:S(2)}) %collective-permute-start.20) | collective-permute-done | bytes 298016 | tf_op jit(solution)/shard_map/ppermute | solution.py:153
  324.2 9.1 %collective-permute-done.21 = bf16[97,768]{1,0:T(8,128)(2,1)S(1)} collective-permute-done((bf16[97,768]{1,0:T(8,128)(2,1)S(1)}, bf16[97,768]{1,0:T(8,128)(2,1)S(1)}, u32[]{:S(2)}, u32[]{:S(2)}) %collective-permute-start.21) | collective-permute-done | bytes 149024 | tf_op jit(solution)/shard_map/ppermute | solution.py:153
  336.5 12.8 %collective-permute-done.22 = bf16[97,768]{1,0:T(8,128)(2,1)S(1)} collective-permute-done((bf16[97,768]{1,0:T(8,128)(2,1)S(1)}, bf16[97,768]{1,0:T(8,128)(2,1)S(1)}, u32[]{:S(2)}, u32[]{:S(2)}) %collective-permute-start.22) | collective-permute-done | bytes 149024 | tf_op jit(solution)/shard_map/ppermute | solution.py:153
  349.5 5.3 %collective-permute-done.29 = bf16[192,768]{1,0:T(8,128)(2,1)S(1)} collective-permute-done((bf16[192,768]{1,0:T(8,128)(2,1)S(1)}, bf16[192,768]{1,0:T(8,128)(2,1)S(1)}, u32[]{:S(2)}, u32[]{:S(2)}) %collective-permute-start.29) | collective-permute-done | bytes 294944 | tf_op jit(solution)/shard_map/ppermute | solution.py:153
  354.9 6.4 %collective-permute-done.23 = bf16[194,768]{1,0:T(8,128)(2,1)S(1)} collective-permute-done((bf16[194,768]{1,0:T(8,128)(2,1)S(1)}, bf16[194,768]{1,0:T(8,128)(2,1)S(1)}, u32[]{:S(2)}, u32[]{:S(2)}) %collective-permute-start.23) | collective-permute-done | bytes 298016 | tf_op jit(solution)/shard_map/ppermute | solution.py:153
  363.2 10.7 %collective-permute-done.30 = bf16[384,768]{1,0:T(8,128)(2,1)S(1)} collective-permute-done((bf16[384,768]{1,0:T(8,128)(2,1)S(1)}, bf16[384,768]{1,0:T(8,128)(2,1)S(1)}, u32[]{:S(2)}, u32[]{:S(2)}) %collective-permute-start.30) | collective-permute-done | bytes 589856 | tf_op jit(solution)/shard_map/ppermute | solution.py:153
  380.9 22.5 %collective-permute-done.31 = bf16[768,768]{1,0:T(8,128)(2,1)} collective-permute-done((bf16[768,768]{1,0:T(8,128)(2,1)}, bf16[768,768]{1,0:T(8,128)(2,1)}, u32[]{:S(2)}, u32[]{:S(2)}) %collective-permute-start.31) | collective-permute-done | bytes 1179680 | tf_op jit(solution)/shard_map/ppermute | solution.py:153
  (328 shorter events, 153.4 us)
Async XLA Ops:
  6.9 15.7 %collective-permute-start.1 = (bf16[2304]{0:T(1024)(128)(2,1)S(1)}, bf16[2304]{0:T(1024)(128)(2,1)S(1)}, u32[]{:S(2)}, u32[]{:S(2)}) collective-permute-start(bf16[2304]{0:T(1024)(128)(2,1)S(1)} %concatenate.153), channel_id=1, source_target_pairs={{0,16},{8,24},{16,0},{24,8},{1,17},{9,25},{17,1},{25,9},{2,18},{10... | collective-permute-start | bytes 13832 | tf_op jit(solution)/shard_map/ppermute | solution.py:153
  14.5 89.1 %collective-permute-start.8 = (bf16[768,768]{1,0:T(8,128)(2,1)}, bf16[768,768]{1,0:T(8,128)(2,1)}, u32[]{:S(2)}, u32[]{:S(2)}) collective-permute-start(bf16[768,768]{1,0:T(8,128)(2,1)} %convert_element_type.299), channel_id=1, source_target_pairs={{0,8},{8,0},{16,24},{24,16},{1,9},{9,1},{17,25},{25,17},{2,10},{10... | collective-permute-start | bytes 3538952 | tf_op jit(solution)/shard_map/ppermute | solution.py:153
  20.3 77.5 %collective-permute-start.11 = (f32[256,768]{1,0:T(8,128)}, f32[256,768]{1,0:T(8,128)}, u32[]{:S(2)}, u32[]{:S(2)}) collective-permute-start(f32[256,768]{1,0:T(8,128)} %get-tuple-element.67), channel_id=1, source_target_pairs={{0,8},{8,0},{16,24},{24,16},{1,9},{9,1},{17,25},{25,17},{2,10},{10... | collective-permute-start | bytes 2359304 | tf_op jit(solution)/shard_map/ppermute | solution.py:153
  28.6 19.6 %collective-permute-start.3 = (bf16[512,768]{1,0:T(8,128)(2,1)S(1)}, bf16[512,768]{1,0:T(8,128)(2,1)S(1)}, u32[]{:S(2)}, u32[]{:S(2)}) collective-permute-start(bf16[512,768]{1,0:T(8,128)(2,1)S(1)} %add_convert_fusion.5), channel_id=1, source_target_pairs={{0,16},{8,24},{16,0},{24,8},{1,17},{9,25},{17,1},{25,9},{2,18},{10... | collective-permute-start | bytes 2359304 | tf_op jit(solution)/shard_map/ppermute | solution.py:153
  74.1 19.1 %collective-permute-start.6 = (bf16[512,768]{1,0:T(8,128)(2,1)}, bf16[512,768]{1,0:T(8,128)(2,1)}, u32[]{:S(2)}, u32[]{:S(2)}) collective-permute-start(bf16[512,768]{1,0:T(8,128)(2,1)} %slice.515), channel_id=1, source_target_pairs={{0,16},{8,24},{16,0},{24,8},{1,17},{9,25},{17,1},{25,9},{2,18},{10... | collective-permute-start | bytes 2359304 | tf_op jit(solution)/shard_map/ppermute | solution.py:153
  97.1 20.8 %collective-permute-start.7 = (bf16[512,768]{1,0:T(8,128)(2,1)}, bf16[512,768]{1,0:T(8,128)(2,1)}, u32[]{:S(2)}, u32[]{:S(2)}) collective-permute-start(bf16[512,768]{1,0:T(8,128)(2,1)} %add_convert_fusion.4), channel_id=1, source_target_pairs={{0,16},{8,24},{16,0},{24,8},{1,17},{9,25},{17,1},{25,9},{2,18},{10... | collective-permute-start | bytes 2359304 | tf_op jit(solution)/shard_map/ppermute | solution.py:153
  100.9 31.1 %collective-permute-start.12 = (bf16[512,768]{1,0:T(8,128)(2,1)}, bf16[512,768]{1,0:T(8,128)(2,1)S(1)}, u32[]{:S(2)}, u32[]{:S(2)}) collective-permute-start(bf16[512,768]{1,0:T(8,128)(2,1)} %get-tuple-element.40), channel_id=1, source_target_pairs={{0,16},{8,24},{16,0},{24,8},{1,17},{9,25},{17,1},{25,9},{2,18},{10... | collective-permute-start | bytes 2359304 | tf_op jit(solution)/shard_map/ppermute | solution.py:153
  144.1 20.5 %collective-permute-start.9 = (bf16[512,768]{1,0:T(8,128)(2,1)S(1)}, bf16[512,768]{1,0:T(8,128)(2,1)S(1)}, u32[]{:S(2)}, u32[]{:S(2)}) collective-permute-start(bf16[512,768]{1,0:T(8,128)(2,1)S(1)} %slice.514), channel_id=1, source_target_pairs={{0,16},{8,24},{16,0},{24,8},{1,17},{9,25},{17,1},{25,9},{2,18},{10... | collective-permute-start | bytes 2359304 | tf_op jit(solution)/shard_map/ppermute | solution.py:153
  145.1 32.8 %collective-permute-start.13 = (bf16[512,768]{1,0:T(8,128)(2,1)S(1)}, bf16[512,768]{1,0:T(8,128)(2,1)S(1)}, u32[]{:S(2)}, u32[]{:S(2)}) collective-permute-start(bf16[512,768]{1,0:T(8,128)(2,1)S(1)} %slice.513), channel_id=1, source_target_pairs={{0,16},{8,24},{16,0},{24,8},{1,17},{9,25},{17,1},{25,9},{2,18},{10... | collective-permute-start | bytes 2359304 | tf_op jit(solution)/shard_map/ppermute | solution.py:153
  183.0 16.3 %collective-permute-start.14 = (bf16[512,768]{1,0:T(8,128)(2,1)}, bf16[512,768]{1,0:T(8,128)(2,1)}, u32[]{:S(2)}, u32[]{:S(2)}) collective-permute-start(bf16[512,768]{1,0:T(8,128)(2,1)} %get-tuple-element.42), channel_id=1, source_target_pairs={{0,16},{8,24},{16,0},{24,8},{1,17},{9,25},{17,1},{25,9},{2,18},{10... | collective-permute-start | bytes 2359304 | tf_op jit(solution)/shard_map/ppermute | solution.py:153
  187.1 76.2 %collective-permute-start.25 = (bf16[1536,768]{1,0:T(8,128)(2,1)}, bf16[1536,768]{1,0:T(8,128)(2,1)}, u32[]{:S(2)}, u32[]{:S(2)}) collective-permute-start(bf16[1536,768]{1,0:T(8,128)(2,1)} %pad_maximum_fusion.2), channel_id=1, source_target_pairs={{0,8},{8,0},{16,24},{24,16},{1,9},{9,1},{17,25},{25,17},{2,10},{10... | collective-permute-start | bytes 7077896 | tf_op jit(solution)/shard_map/ppermute | solution.py:153
  191.8 75.1 %collective-permute-start.10 = (f32[256,768]{1,0:T(8,128)}, f32[256,768]{1,0:T(8,128)}, u32[]{:S(2)}, u32[]{:S(2)}) collective-permute-start(f32[256,768]{1,0:T(8,128)} %slice.409), channel_id=1, source_target_pairs={{0,8},{8,0},{16,24},{24,16},{1,9},{9,1},{17,25},{25,17},{2,10},{10... | collective-permute-start | bytes 2359304 | tf_op jit(solution)/shard_map/ppermute | solution.py:153
  263.2 16.6 %collective-permute-start.18 = (bf16[776,768]{1,0:T(8,128)(2,1)}, bf16[776,768]{1,0:T(8,128)(2,1)}, u32[]{:S(2)}, u32[]{:S(2)}) collective-permute-start(bf16[776,768]{1,0:T(8,128)(2,1)} %constant_dynamic-update-slice_fusion.10), channel_id=1, source_target_pairs={{0,8},{8,0},{16,24},{24,16},{1,9},{9,1},{17,25},{25,17},{2,10},{10... | collective-permute-start | bytes 3575816 | tf_op jit(solution)/shard_map/ppermute | solution.py:153
  265.9 28.9 %collective-permute-start.26 = (bf16[768,768]{1,0:T(8,128)(2,1)S(1)}, bf16[768,768]{1,0:T(8,128)(2,1)}, u32[]{:S(2)}, u32[]{:S(2)}) collective-permute-start(bf16[768,768]{1,0:T(8,128)(2,1)S(1)} %constant_dynamic-slice_fusion.2), channel_id=1, source_target_pairs={{0,1},{1,0},{2,3},{3,2},{4,5},{5,4},{6,7},{7,6},{8,9},{9,8},{10,11... | collective-permute-start | bytes 3538952 | tf_op jit(solution)/shard_map/ppermute | solution.py:153
  282.1 25.2 %collective-permute-start.19 = (bf16[388,768]{1,0:T(8,128)(2,1)S(1)}, bf16[388,768]{1,0:T(8,128)(2,1)S(1)}, u32[]{:S(2)}, u32[]{:S(2)}) collective-permute-start(bf16[388,768]{1,0:T(8,128)(2,1)S(1)} %constant_dynamic-slice_fusion.5), channel_id=1, source_target_pairs={{0,1},{1,0},{2,3},{3,2},{4,5},{5,4},{6,7},{7,6},{8,9},{9,8},{10,11... | collective-permute-start | bytes 1787912 | tf_op jit(solution)/shard_map/ppermute | solution.py:153
  296.5 15.7 %collective-permute-start.27 = (bf16[384,768]{1,0:T(8,128)(2,1)S(1)}, bf16[384,768]{1,0:T(8,128)(2,1)S(1)}, u32[]{:S(2)}, u32[]{:S(2)}) collective-permute-start(bf16[384,768]{1,0:T(8,128)(2,1)S(1)} %constant_dynamic-slice_fusion.1), channel_id=1, source_target_pairs={{0,2},{1,3},{2,0},{3,1},{4,6},{5,7},{6,4},{7,5},{8,10},{9,11},{10,... | collective-permute-start | bytes 1769480 | tf_op jit(solution)/shard_map/ppermute | solution.py:153
  307.6 15.6 %collective-permute-start.20 = (bf16[194,768]{1,0:T(8,128)(2,1)S(1)}, bf16[194,768]{1,0:T(8,128)(2,1)S(1)}, u32[]{:S(2)}, u32[]{:S(2)}) collective-permute-start(bf16[194,768]{1,0:T(8,128)(2,1)S(1)} %constant_dynamic-slice_fusion.4), channel_id=1, source_target_pairs={{0,2},{1,3},{2,0},{3,1},{4,6},{5,7},{6,4},{7,5},{8,10},{9,11},{10,... | collective-permute-start | bytes 893960 | tf_op jit(solution)/shard_map/ppermute | solution.py:153
  312.5 21.0 %collective-permute-start.28 = (bf16[192,768]{1,0:T(8,128)(2,1)S(1)}, bf16[192,768]{1,0:T(8,128)(2,1)S(1)}, u32[]{:S(2)}, u32[]{:S(2)}) collective-permute-start(bf16[192,768]{1,0:T(8,128)(2,1)S(1)} %constant_dynamic-slice_fusion), channel_id=1, source_target_pairs={{0,4},{1,5},{2,6},{3,7},{4,0},{5,1},{6,2},{7,3},{8,12},{9,13},{10,... | collective-permute-start | bytes 884744 | tf_op jit(solution)/shard_map/ppermute | solution.py:153
  324.2 38.9 %collective-permute-start.16 = (f32[256,768]{1,0:T(8,128)S(1)}, f32[256,768]{1,0:T(8,128)S(1)}, u32[]{:S(2)}, u32[]{:S(2)}) collective-permute-start(f32[256,768]{1,0:T(8,128)S(1)} %slice.415), channel_id=1, source_target_pairs={{0,8},{8,0},{16,24},{24,16},{1,9},{9,1},{17,25},{25,17},{2,10},{10... | collective-permute-start | bytes 2359304 | tf_op jit(solution)/shard_map/ppermute | solution.py:153
  333.4 15.9 %collective-permute-start.22 = (bf16[97,768]{1,0:T(8,128)(2,1)S(1)}, bf16[97,768]{1,0:T(8,128)(2,1)S(1)}, u32[]{:S(2)}, u32[]{:S(2)}) collective-permute-start(bf16[97,768]{1,0:T(8,128)(2,1)S(1)} %add_convert_fusion.10), channel_id=1, source_target_pairs={{0,4},{1,5},{2,6},{3,7},{4,0},{5,1},{6,2},{7,3},{8,12},{9,13},{10,... | collective-permute-start | bytes 446984 | tf_op jit(solution)/shard_map/ppermute | solution.py:153
  333.6 21.2 %collective-permute-start.29 = (bf16[192,768]{1,0:T(8,128)(2,1)S(1)}, bf16[192,768]{1,0:T(8,128)(2,1)S(1)}, u32[]{:S(2)}, u32[]{:S(2)}) collective-permute-start(bf16[192,768]{1,0:T(8,128)(2,1)S(1)} %add_convert_fusion.9), channel_id=1, source_target_pairs={{0,4},{1,5},{2,6},{3,7},{4,0},{5,1},{6,2},{7,3},{8,12},{9,13},{10,... | collective-permute-start | bytes 884744 | tf_op jit(solution)/shard_map/ppermute | solution.py:153
  354.8 19.0 %collective-permute-start.30 = (bf16[384,768]{1,0:T(8,128)(2,1)S(1)}, bf16[384,768]{1,0:T(8,128)(2,1)S(1)}, u32[]{:S(2)}, u32[]{:S(2)}) collective-permute-start(bf16[384,768]{1,0:T(8,128)(2,1)S(1)} %pad_maximum_fusion.30), channel_id=1, source_target_pairs={{0,2},{1,3},{2,0},{3,1},{4,6},{5,7},{6,4},{7,5},{8,10},{9,11},{10,... | collective-permute-start | bytes 1769480 | tf_op jit(solution)/shard_map/ppermute | solution.py:153
  361.5 16.4 %collective-permute-start.24 = (bf16[388,768]{1,0:T(8,128)(2,1)S(1)}, bf16[388,768]{1,0:T(8,128)(2,1)S(1)}, u32[]{:S(2)}, u32[]{:S(2)}) collective-permute-start(bf16[388,768]{1,0:T(8,128)(2,1)S(1)} %pad_maximum_fusion.28), channel_id=1, source_target_pairs={{0,1},{1,0},{2,3},{3,2},{4,5},{5,4},{6,7},{7,6},{8,9},{9,8},{10,11... | collective-permute-start | bytes 1787912 | tf_op jit(solution)/shard_map/ppermute | solution.py:153
  375.2 28.2 %collective-permute-start.31 = (bf16[768,768]{1,0:T(8,128)(2,1)}, bf16[768,768]{1,0:T(8,128)(2,1)}, u32[]{:S(2)}, u32[]{:S(2)}) collective-permute-start(bf16[768,768]{1,0:T(8,128)(2,1)} %pad_maximum_fusion.18), channel_id=1, source_target_pairs={{0,1},{1,0},{2,3},{3,2},{4,5},{5,4},{6,7},{7,6},{8,9},{9,8},{10,11... | collective-permute-start | bytes 3538952 | tf_op jit(solution)/shard_map/ppermute | solution.py:153
  (54 other events, 685.2 us)
